TPU v7x, 32 devices: a whole 2x2x4 slice. The times are simulated.
32 devices in a mesh: fsdp: 4 (over z), context: 2 (over y), tensor: 4 (over x, core).
Axes of the slice: x: 2, y: 2, z: 4, core: 2. Of those that a mesh axis runs over, the one named last changes fastest.
Arguments:
- inputs: float32 [4, 512, 1024], P('fsdp', 'context'), may hold values from -6 to 6
- block_len: int32 [4, 2], P('fsdp'), may hold values from 1 to 256, as said below
- leading_norm_gain: float32 [1024], replicated, may hold values from 0.1 to 1.9
- leading_norm_bias: float32 [1024], replicated, may hold values from -2 to 2
- qkv_weight: bfloat16 [1024, 3, 1024], P('fsdp', None, 'tensor'), may hold values from -1 to 1
- qv_bias: float32 [2, 1024], P(None, 'tensor'), may hold values from -3 to 3
- out_weight: bfloat16 [1024, 1024], P('fsdp', 'tensor'), may hold values from -4 to 4
- out_bias: float32 [1024], replicated, may hold values from -2 to 2
- middle_norm_gain: float32 [1024], replicated, may hold values from 0.1 to 1.9
- middle_norm_bias: float32 [1024], replicated, may hold values from -2 to 2
- up_weight: bfloat16 [1024, 4096], P('fsdp', 'tensor'), may hold values from -0.1875 to 0.1875
- up_bias: float32 [4096], P('tensor'), may hold values from -3 to 3
- down_weight: bfloat16 [1024, 4096], P('fsdp', 'tensor'), may hold values from -0.09375 to 0.09375
- down_bias: float32 [1024], replicated, may hold values from -2 to 2
- cotangent: float32 [4, 512, 1024], P('fsdp', 'context'), may hold values from -6 to 6
Outputs:
- outputs: float32 [4, 512, 1024], P('fsdp', 'context')
- grad_inputs: float32 [4, 512, 1024], P('fsdp', 'context')
- grad_pre_gain: float32 [1024], replicated
- grad_pre_shift: float32 [1024], replicated
- grad_qkv_weight: float32 [1024, 3, 1024], P('fsdp', None, 'tensor')
- grad_qv_bias: float32 [2, 1024], P(None, 'tensor')
- grad_out_weight: float32 [1024, 1024], P('fsdp', 'tensor')
- grad_out_bias: float32 [1024], replicated
- grad_mid_gain: float32 [1024], replicated
- grad_mid_shift: float32 [1024], replicated
- grad_up_weight: float32 [1024, 4096], P('fsdp', 'tensor')
- grad_up_bias: float32 [4096], P('tensor')
- grad_down_weight: float32 [1024, 4096], P('fsdp', 'tensor')
- grad_down_bias: float32 [1024], replicated
Inputs may be any that keep to these rules, and one draw needn't show every extreme that they name: `block_len`: the live tokens of the 2 blocks of an image add up to 384, and one block of every image holds exactly 256.
All inputs are finite; a program needn't handle non-finite values.
Results may differ from a plain program's by a relative error of at most 0.02.
Values may be sent and summed in bfloat16 or wider, within the bound.
A program may use at most 128 MiB of HBM per device.

v0:
```python
import math
import jax
import jax.numpy as jnp
from jax import lax
from jax.sharding import PartitionSpec as P

HD = 64
EPS = 1e-06
SQRT_HALF = 0.7071067811865476
INV_ROOT_TAU = 0.3989422804014327
NEG_BIG = -1e30


def layer_norm_forward(rows, norm_gain, norm_bias):
    centered_rows = rows - jnp.mean(rows, axis=-1, keepdims=True)
    inverse_deviation = lax.rsqrt(
        jnp.mean(centered_rows * centered_rows, axis=-1, keepdims=True) + EPS
    )
    normalized_rows = centered_rows * inverse_deviation
    return (normalized_rows * norm_gain + norm_bias, normalized_rows, inverse_deviation)


def layer_norm_backward(output_gradient, normalized_rows, inverse_deviation, norm_gain):
    scaled_rows = output_gradient * norm_gain
    return inverse_deviation * (
        scaled_rows
        - jnp.mean(scaled_rows, axis=-1, keepdims=True)
        - normalized_rows * jnp.mean(scaled_rows * normalized_rows, axis=-1, keepdims=True)
    )


def gelu_value(value):
    return 0.5 * value * (1.0 + lax.erf(value * SQRT_HALF))


def gelu_slope(value):
    return 0.5 * (1.0 + lax.erf(value * SQRT_HALF)) + value * INV_ROOT_TAU * jnp.exp(
        -0.5 * value * value
    )


def key_live(start, count, lengths, block_rows):
    slots = start + jnp.arange(count, dtype=jnp.int32)
    owner = slots // block_rows
    table = jnp.arange(lengths.shape[0], dtype=jnp.int32)
    limit = jnp.sum(jnp.where(owner[:, None] == table[None, :], lengths[None, :], 0), axis=1)
    return slots % block_rows < limit


def attend_block(state, block, queries, lengths, block_rows, score_scale):
    peak, total, accum = state
    key_rows, value_rows, start = block
    live_keys = key_live(start, key_rows.shape[0], lengths, block_rows)
    scores = (
        jnp.einsum("qhe,khe->qhk", queries, key_rows, preferred_element_type=jnp.float32)
        * score_scale
    )
    scores = jnp.where(live_keys[None, None, :], scores, NEG_BIG)
    new_peak = jnp.maximum(peak, jnp.max(scores, axis=2))
    weights = jnp.where(live_keys[None, None, :], jnp.exp(scores - new_peak[:, :, None]), 0.0)
    decay = jnp.exp(peak - new_peak)
    total = total * decay + jnp.sum(weights, axis=2)
    accum = accum * decay[:, :, None] + jnp.einsum(
        "qhk,khe->qhe", weights.astype(jnp.bfloat16), value_rows, preferred_element_type=jnp.float32
    )
    return (new_peak, total, accum)


def attend_piece(state, piece, queries, lengths, block_rows, score_scale):
    key_piece, value_piece = piece
    count = key_piece.shape[0] // block_rows
    heads_local = queries.shape[1]
    key_blocks = key_piece.reshape(count, block_rows, heads_local, HD)
    value_blocks = value_piece.reshape(count, block_rows, heads_local, HD)
    starts = block_rows * jnp.arange(count, dtype=jnp.int32)

    def advance(carry, block):
        return (attend_block(carry, block, queries, lengths, block_rows, score_scale), None)

    state, unused = lax.scan(advance, state, (key_blocks, value_blocks, starts))
    return state


def local(
    inputs,
    block_len,
    leading_norm_gain,
    leading_norm_bias,
    qkv_weight,
    qv_bias,
    out_weight,
    out_bias,
    middle_norm_gain,
    middle_norm_bias,
    up_weight,
    up_bias,
    down_weight,
    down_bias,
    cotangent,
):
    incoming_rows = inputs[0]
    block_rows = incoming_rows.shape[0]
    lengths = block_len[0]
    blocks_count = lengths.shape[0]
    score_scale = 1.0 / math.sqrt(HD)
    position = lax.axis_index("context")
    own_length = jnp.sum(
        jnp.where(jnp.arange(blocks_count, dtype=jnp.int32) == position, lengths, 0)
    )
    live = (jnp.arange(block_rows, dtype=jnp.int32) < own_length).astype(jnp.float32)[:, None]
    qkv_full, out_full, up_full, down_full = (
        lax.all_gather(qkv_weight, "fsdp", axis=0, tiled=True),
        lax.all_gather(out_weight, "fsdp", axis=0, tiled=True),
        lax.all_gather(up_weight, "fsdp", axis=0, tiled=True),
        lax.all_gather(down_weight, "fsdp", axis=0, tiled=True),
    )
    width = qkv_full.shape[0]
    local_width = qkv_full.shape[2]
    heads_local = local_width // HD
    qkv_flat = qkv_full.reshape(width, 3 * local_width)
    first_normed, first_normalized, first_inverse_deviation = layer_norm_forward(
        incoming_rows, leading_norm_gain, leading_norm_bias
    )
    norm1_b = first_normed.astype(jnp.bfloat16)
    projected = jnp.dot(norm1_b, qkv_flat, preferred_element_type=jnp.float32).reshape(
        block_rows, 3, local_width
    )
    queries = (projected[:, 0] + qv_bias[0]).astype(jnp.bfloat16)
    keys = projected[:, 1].astype(jnp.bfloat16)
    values = (projected[:, 2] + qv_bias[1]).astype(jnp.bfloat16)
    query_heads = queries.reshape(block_rows, heads_local, HD)
    start_state = (
        jnp.full((block_rows, heads_local), NEG_BIG, jnp.float32),
        jnp.zeros((block_rows, heads_local), jnp.float32),
        jnp.zeros((block_rows, heads_local, HD), jnp.float32),
    )
    peak, total, accum = attend_piece(
        start_state,
        (
            lax.all_gather(keys, "context", axis=0, tiled=True),
            lax.all_gather(values, "context", axis=0, tiled=True),
        ),
        query_heads,
        lengths,
        block_rows,
        score_scale,
    )
    attn_heads = accum / total[:, :, None]
    lse = peak + jnp.log(total)
    attn_b = attn_heads.reshape(block_rows, local_width).astype(jnp.bfloat16)
    attn_part = jnp.dot(attn_b, out_full.T, preferred_element_type=jnp.float32)
    residual_rows = (
        incoming_rows
        + lax.psum(attn_part.astype(jnp.bfloat16), "tensor").astype(jnp.float32)
        + out_bias
    )
    second_normed, second_normalized, second_inverse_deviation = layer_norm_forward(
        residual_rows, middle_norm_gain, middle_norm_bias
    )
    norm2_b = second_normed.astype(jnp.bfloat16)
    pre_act = jnp.dot(norm2_b, up_full, preferred_element_type=jnp.float32) + up_bias
    hidden = gelu_value(pre_act).astype(jnp.bfloat16)
    mlp_part = jnp.dot(hidden, down_full.T, preferred_element_type=jnp.float32)
    result = live * (
        residual_rows
        + lax.psum(mlp_part.astype(jnp.bfloat16), "tensor").astype(jnp.float32)
        + down_bias
    )
    result_gradient = live * cotangent[0]
    grad_y_b = result_gradient.astype(jnp.bfloat16)
    down_weight_gradient = jnp.dot(grad_y_b.T, hidden, preferred_element_type=jnp.float32)
    hidden_gradient = jnp.dot(grad_y_b, down_full, preferred_element_type=jnp.float32) * gelu_slope(
        pre_act
    )
    grad_u_b = hidden_gradient.astype(jnp.bfloat16)
    up_weight_gradient = jnp.dot(norm2_b.T, grad_u_b, preferred_element_type=jnp.float32)
    second_norm_gradient = lax.psum(
        jnp.dot(grad_u_b, up_full.T, preferred_element_type=jnp.float32).astype(jnp.bfloat16),
        "tensor",
    ).astype(jnp.float32)
    residual_gradient = result_gradient + layer_norm_backward(
        second_norm_gradient, second_normalized, second_inverse_deviation, middle_norm_gain
    )
    grad_resid_b = residual_gradient.astype(jnp.bfloat16)
    out_weight_gradient = jnp.dot(grad_resid_b.T, attn_b, preferred_element_type=jnp.float32)
    grad_attn = jnp.dot(grad_resid_b, out_full, preferred_element_type=jnp.float32).astype(
        jnp.bfloat16
    )
    grad_attn_heads = grad_attn.reshape(block_rows, heads_local, HD)
    delta = jnp.sum(grad_attn_heads.astype(jnp.float32) * attn_heads, axis=2)
    all_keys, all_values = (
        lax.all_gather(keys, "context", axis=0, tiled=True),
        lax.all_gather(values, "context", axis=0, tiled=True),
    )
    key_blocks = all_keys.reshape(blocks_count, block_rows, heads_local, HD)
    value_blocks = all_values.reshape(blocks_count, block_rows, heads_local, HD)
    starts = block_rows * jnp.arange(blocks_count, dtype=jnp.int32)

    def back_block(grad_query, block):
        key_rows, value_rows, start = block
        live_keys = key_live(start, key_rows.shape[0], lengths, block_rows)
        scores = (
            jnp.einsum("qhe,khe->qhk", query_heads, key_rows, preferred_element_type=jnp.float32)
            * score_scale
        )
        probs = jnp.where(live_keys[None, None, :], jnp.exp(scores - lse[:, :, None]), 0.0)
        grad_value = jnp.einsum(
            "qhk,qhe->khe",
            probs.astype(jnp.bfloat16),
            grad_attn_heads,
            preferred_element_type=jnp.float32,
        )
        grad_probs = jnp.einsum(
            "qhe,khe->qhk", grad_attn_heads, value_rows, preferred_element_type=jnp.float32
        )
        grad_scores = (probs * (grad_probs - delta[:, :, None])).astype(jnp.bfloat16)
        grad_query = grad_query + score_scale * jnp.einsum(
            "qhk,khe->qhe", grad_scores, key_rows, preferred_element_type=jnp.float32
        )
        grad_key = score_scale * jnp.einsum(
            "qhk,qhe->khe", grad_scores, query_heads, preferred_element_type=jnp.float32
        )
        return (grad_query, (grad_key, grad_value))

    grad_query_heads, stacked = lax.scan(
        back_block,
        jnp.zeros((block_rows, heads_local, HD), jnp.float32),
        (key_blocks, value_blocks, starts),
    )
    key_terms = stacked[0].reshape(blocks_count * block_rows, local_width)
    value_terms = stacked[1].reshape(blocks_count * block_rows, local_width)
    grad_keys, values_gradient = (
        lax.psum_scatter(
            key_terms.astype(jnp.bfloat16), "context", scatter_dimension=0, tiled=True
        ).astype(jnp.float32),
        lax.psum_scatter(
            value_terms.astype(jnp.bfloat16), "context", scatter_dimension=0, tiled=True
        ).astype(jnp.float32),
    )
    queries_gradient = grad_query_heads.reshape(block_rows, local_width)
    grad_p = (
        jnp.stack([queries_gradient, grad_keys, values_gradient], axis=1)
        .astype(jnp.bfloat16)
        .reshape(block_rows, 3 * local_width)
    )
    query_key_value_weight_gradient = jnp.dot(
        norm1_b.T, grad_p, preferred_element_type=jnp.float32
    ).reshape(width, 3, local_width)
    first_norm_gradient = lax.psum(
        jnp.dot(grad_p, qkv_flat.T, preferred_element_type=jnp.float32).astype(jnp.bfloat16),
        "tensor",
    ).astype(jnp.float32)
    input_gradient = residual_gradient + layer_norm_backward(
        first_norm_gradient, first_normalized, first_inverse_deviation, leading_norm_gain
    )
    small_terms = (
        jnp.sum(first_norm_gradient * first_normalized, axis=0),
        jnp.sum(first_norm_gradient, axis=0),
        jnp.stack([jnp.sum(queries_gradient, axis=0), jnp.sum(values_gradient, axis=0)]),
        jnp.sum(residual_gradient, axis=0),
        jnp.sum(second_norm_gradient * second_normalized, axis=0),
        jnp.sum(second_norm_gradient, axis=0),
        jnp.sum(hidden_gradient, axis=0),
        jnp.sum(result_gradient, axis=0),
    )
    small = lax.psum(
        (
            small_terms[0],
            small_terms[1],
            small_terms[2],
            small_terms[3],
            small_terms[4],
            small_terms[5],
            small_terms[6],
            small_terms[7],
        ),
        ("fsdp", "context"),
    )
    weight_terms = (
        query_key_value_weight_gradient,
        out_weight_gradient,
        up_weight_gradient,
        down_weight_gradient,
    )
    owned = (
        lax.psum_scatter(
            weight_terms[0].astype(jnp.bfloat16), "fsdp", scatter_dimension=0, tiled=True
        ).astype(jnp.float32),
        lax.psum_scatter(
            weight_terms[1].astype(jnp.bfloat16), "fsdp", scatter_dimension=0, tiled=True
        ).astype(jnp.float32),
        lax.psum_scatter(
            weight_terms[2].astype(jnp.bfloat16), "fsdp", scatter_dimension=0, tiled=True
        ).astype(jnp.float32),
        lax.psum_scatter(
            weight_terms[3].astype(jnp.bfloat16), "fsdp", scatter_dimension=0, tiled=True
        ).astype(jnp.float32),
    )
    summed = (
        lax.psum(owned[0].astype(jnp.bfloat16), "context").astype(jnp.float32),
        lax.psum(owned[1].astype(jnp.bfloat16), "context").astype(jnp.float32),
        lax.psum(owned[2].astype(jnp.bfloat16), "context").astype(jnp.float32),
        lax.psum(owned[3].astype(jnp.bfloat16), "context").astype(jnp.float32),
    )
    return (
        result[None],
        input_gradient[None],
        small[0],
        small[1],
        summed[0],
        small[2],
        summed[1],
        small[3],
        small[4],
        small[5],
        summed[2],
        small[6],
        summed[3],
        small[7],
    )


def solution(mesh):
    in_specs = (
        P("fsdp", "context", None),
        P("fsdp", None),
        P(),
        P(),
        P("fsdp", None, "tensor"),
        P(None, "tensor"),
        P("fsdp", "tensor"),
        P(),
        P(),
        P(),
        P("fsdp", "tensor"),
        P("tensor"),
        P("fsdp", "tensor"),
        P(),
        P("fsdp", "context", None),
    )
    out_specs = (
        P("fsdp", "context", None),
        P("fsdp", "context", None),
        P(),
        P(),
        P("fsdp", None, "tensor"),
        P(None, "tensor"),
        P("fsdp", "tensor"),
        P(),
        P(),
        P(),
        P("fsdp", "tensor"),
        P("tensor"),
        P("fsdp", "tensor"),
        P(),
    )
    return jax.shard_map(local, mesh=mesh, in_specs=in_specs, out_specs=out_specs, check_vma=False)
```

profile of v0, /device:TPU:0, one launch (start us, length us, event | category | flops | bytes accessed | tf_op | source)
XLA Modules:
  0.0 550.5 jit_solution(16767555452843351469)
XLA Ops:
  10.6 22.1 %all_gather.23 = bf16[1024,256]{1,0:T(8,128)(2,1)S(1)} all-gather(bf16[256,256]{1,0:T(8,128)(2,1)S(1)} %copy-done.21), channel_id=1, replica_groups=mesh['fsdp'=4,'context'=2,'tensor'=4] {'fsdp'}, dimensions={0}, use_global_device_ids=true | all-gather | bytes 655360 | tf_op jit(solution)/shard_map/all_gather | solution.py:113
  32.6 19.6 %all-gather.5.cloned.1.call-done = bf16[1024,3,256]{2,0,1:T(8,128)(2,1)} async-done(((bf16[256,3,256]{2,0,1:T(8,128)(2,1)}), bf16[1024,3,256]{2,0,1:T(8,128)(2,1)}) %all-gather.5.cloned.1.call-update) | async-done | bytes 1572880 | tf_op jit(solution)/shard_map/all_gather | solution.py:112
  57.1 6.0 %all_gather.22 = bf16[512,256]{0,1:T(8,128)(2,1)S(1)} all-gather(bf16[256,256]{0,1:T(8,128)(2,1)S(1)} %fusion.75), channel_id=1, replica_groups=mesh['fsdp'=4,'context'=2,'tensor'=4] {'context'}, dimensions={0}, use_global_device_ids=true | all-gather | bytes 393216 | tf_op jit(solution)/shard_map/all_gather | solution.py:141
  63.2 5.6 %all-gather = bf16[512,1,256]{0,2,1:T(8,128)(2,1)S(1)} all-gather(bf16[256,1,256]{0,2,1:T(8,128)(2,1)S(1)} %slice.31), channel_id=2, replica_groups=mesh['fsdp'=4,'context'=2,'tensor'=4] {'context'}, dimensions={0}, use_global_device_ids=true | all-gather | bytes 393216 | tf_op jit(solution)/shard_map/all_gather | solution.py:140
  69.0 5.9 %while.34 = (s32[]{:T(128)}, f32[256,4]{0,1:T(4,128)S(1)}, f32[256,4]{0,1:T(4,128)S(1)}, f32[256,4,64]{0,2,1:T(8,128)S(1)}, s32[2]{0:T(128)S(1)}, /*index=5*/s32...) while((s32[]{:T(128)}, f32[256,4]{0,1:T(4,128)S(1)}, ...), condition=%wide.region_7.8_spmd.clone, body=%wide.region_3.7_spmd.clone.sunk | while | flops 69678592 | bytes 4134565 | solution.py:80
  79.5 30.9 %all-reduce.8.cloned.1.call-done = bf16[256,1024]{1,0:T(8,128)(2,1)} async-done(((bf16[256,1024]{1,0:T(8,128)(2,1)}), bf16[256,1024]{1,0:T(8,128)(2,1)}) %all-reduce.8.cloned.1.call-update) | async-done | bytes 524304 | tf_op jit(solution)/shard_map/psum | solution.py:154
  112.0 45.8 %all-gather.7.cloned.1.call-done = bf16[1024,1024]{1,0:T(8,128)(2,1)} async-done(((bf16[256,1024]{1,0:T(8,128)(2,1)}), bf16[1024,1024]{1,0:T(8,128)(2,1)}) %all-gather.7.cloned.1.call-update) | async-done | bytes 2097168 | tf_op jit(solution)/shard_map/all_gather | solution.py:114
  157.8 3.3 convolution_add_fusion
  161.1 42.6 %all-gather.9.cloned.1.call-done = bf16[1024,1024]{1,0:T(8,128)(2,1)} async-done(((bf16[256,1024]{1,0:T(8,128)(2,1)}), bf16[1024,1024]{1,0:T(8,128)(2,1)}) %all-gather.9.cloned.1.call-update) | async-done | bytes 2097168 | tf_op jit(solution)/shard_map/all_gather | solution.py:115
  203.7 3.6 fusion.92
  210.3 31.7 %all-reduce.10.cloned.1.call-done = bf16[256,1024]{1,0:T(8,128)(2,1)} async-done(((bf16[256,1024]{1,0:T(8,128)(2,1)}), bf16[256,1024]{1,0:T(8,128)(2,1)}) %all-reduce.10.cloned.1.call-update) | async-done | bytes 524304 | tf_op jit(solution)/shard_map/psum | solution.py:177
  247.2 14.2 %while.35 = (s32[]{:T(128)}, f32[256,4,64]{0,2,1:T(8,128)}, bf16[2,256,4,64]{1,3,2,0:T(8,128)(2,1)}, bf16[2,256,4,64]{1,3,2,0:T(8,128)(2,1)}, bf16[2,256,4,64]{1...) while((s32[]{:T(128)}, f32[256,4,64]{0,2,1:T(8,128)}, ...), condition=%wide.region_18.19_spmd.clone, body=%wide.region_16.18_spmd.clone.sunk | while | flops 169878016 | bytes 12989295 | solution.py:225
  271.3 6.4 %reduce-scatter.9.cloned.1.call-done = bf16[256,256]{1,0:T(8,128)(2,1)} async-done(((bf16[512,256]{1,0:T(8,128)(2,1)}), bf16[256,256]{1,0:T(8,128)(2,1)}) %reduce-scatter.9.cloned.1.call-update) | async-done | bytes 131088 | tf_op jit(solution)/shard_map/reduce_scatter | solution.py:236
  277.6 14.6 %reduce-scatter.7.cloned.1.call-done = bf16[256,256]{1,0:T(8,128)(2,1)} async-done(((bf16[512,256]{1,0:T(8,128)(2,1)}), bf16[256,256]{1,0:T(8,128)(2,1)}) %reduce-scatter.7.cloned.1.call-update) | async-done | bytes 131088 | tf_op jit(solution)/shard_map/reduce_scatter | solution.py:233
  299.2 3.2 convolution_convert_fusion.1
  302.5 3.7 convolution_convert_fusion
  306.3 3.6 convolution_convert_fusion.6
  311.4 5.5 %reduce-scatter.13.cloned.1.call-done = bf16[256,256]{1,0:T(8,128)(2,1)} async-done(((bf16[1024,256]{1,0:T(8,128)(2,1)}), bf16[256,256]{1,0:T(8,128)(2,1)}) %reduce-scatter.13.cloned.1.call-update) | async-done | bytes 131088 | tf_op jit(solution)/shard_map/reduce_scatter | solution.py:289
  317.0 36.0 %reduce-scatter.11.cloned.1.call-done = bf16[256,3,256]{2,0,1:T(8,128)(2,1)} async-done(((bf16[1024,3,256]{2,0,1:T(8,128)(2,1)}), bf16[256,3,256]{2,0,1:T(8,128)(2,1)}) %reduce-scatter.11.cloned.1.call-update) | async-done | bytes 393232 | tf_op jit(solution)/shard_map/reduce_scatter | solution.py:286
  352.9 44.6 %reduce-scatter.15.cloned.1.call-done = bf16[256,1024]{1,0:T(8,128)(2,1)} async-done(((bf16[1024,1024]{1,0:T(8,128)(2,1)}), bf16[256,1024]{1,0:T(8,128)(2,1)}) %reduce-scatter.15.cloned.1.call-update) | async-done | bytes 524304 | tf_op jit(solution)/shard_map/reduce_scatter | solution.py:292
  397.6 45.2 %reduce-scatter.17.cloned.1.call-done = bf16[256,1024]{1,0:T(8,128)(2,1)} async-done(((bf16[1024,1024]{1,0:T(8,128)(2,1)}), bf16[256,1024]{1,0:T(8,128)(2,1)}) %reduce-scatter.17.cloned.1.call-update) | async-done | bytes 524304 | tf_op jit(solution)/shard_map/reduce_scatter | solution.py:295
  444.3 37.4 %all-reduce.12.cloned.1.call-done = (bf16[256,1024]{1,0:T(8,128)(2,1)}, bf16[256,1024]{1,0:T(8,128)(2,1)}) async-done(((bf16[256,1024]{1,0:T(8,128)(2,1)}, bf16[256,1024]{1,0:T(8,128)(2,1)}), (bf16[256,1024]{1,0:T(8,128)(2,1)}, bf16[256,1024]{1,0:T(8,128)(2,1)})) %all-reduce.12.cloned.1.call-update) | async-done | bytes 1048592 | tf_op jit(solution)/shard_map/psum | solution.py:166
  483.3 38.9 %all-reduce = (f32[1024]{0:T(1024)}, f32[1024]{0:T(1024)}, f32[2,256]{1,0:T(2,128)}, f32[1024]{0:T(1024)}, f32[1024]{0:T(1024)}, /*index=5*/f32[1024]{0:T(1024)}, f32[1024]{0:T(1024)}, f32[1024]{0:T(1024)}) all-reduce(f32[1024]{0:T(1024)S(1)} %get-tuple-element.426, ...), channel_id=1, replica_groups=mesh['fsdp'=4,'context'=2,'tensor'=4] {'fsdp','context'}, use_global_device_ids=true, to_apply=%region_25.26 | all-reduce | flops 7680 | bytes 61440 | tf_op jit(solution)/shard_map/psum | solution.py:266
  525.8 11.4 %all-reduce.14.cloned.1.call-done = (bf16[256,3,256]{2,0,1:T(8,128)(2,1)}, bf16[256,256]{1,0:T(8,128)(2,1)}, bf16[256,1024]{1,0:T(8,128)(2,1)}, bf16[256,1024]{1,0:T(8,128)(2,1)}) async-done(((bf16[256,3,256]{2,0,1:T(8,128)(2,1)}, bf16[256,256]{1,0:T(8,128)(2,1)}, bf16[256,1024]{1,0:T(8,128)(2,1)}, bf16[256,1024]{1,0:T(8,128)(2,1)}), (bf16[256,3,256]{2,0,1:T(8,128)(2,1)}, bf16[256,256]{1,0:T(8,128)(2,1)}, ...) | async-done | bytes 1572880 | tf_op jit(solution)/shard_map/psum | solution.py:300
  (220 shorter events, 74.2 us)
Async XLA Ops:
  7.2 45.0 %all-gather.5.cloned.1.call-start = ((), (), s32[]{:S(2)}) async-start(), calls=%async_computation.6 | async-start | bytes 1966080 | tf_op jit(solution)/shard_map/all_gather | solution.py:112
  7.9 102.5 %all-reduce.8.cloned.1.call-start = ((), (), s32[]{:S(2)}) async-start(), calls=%async_computation.7 | async-start | bytes 1048576 | tf_op jit(solution)/shard_map/psum | solution.py:154
  10.3 44.5 %copy-start.27 = (f32[256]{0:T(256)}, f32[256]{0:T(256)S(1)}, u32[]{:S(2)}) copy-start(f32[256]{0:T(256)S(1)} %broadcast_multiply_fusion.5) | copy-start | bytes 3076
  76.8 81.0 %all-gather.7.cloned.1.call-start = ((), (), s32[]{:S(2)}) async-start(), calls=%async_computation.8 | async-start | bytes 2621440 | tf_op jit(solution)/shard_map/all_gather | solution.py:114
  77.5 80.2 %copy-start.25 = (f32[1024]{0:T(1024)S(1)}, f32[1024]{0:T(1024)}, u32[]{:S(2)}) copy-start(f32[1024]{0:T(1024)} %param.27) | copy-start | bytes 12292
  77.5 80.2 %copy-start.38 = (f32[1024]{0:T(1024)S(1)}, f32[1024]{0:T(1024)}, u32[]{:S(2)}) copy-start(f32[1024]{0:T(1024)} %param.28) | copy-start | bytes 12292
  77.6 80.2 %copy-start.40 = (f32[1024]{0:T(1024)S(1)}, f32[1024]{0:T(1024)}, u32[]{:S(2)}) copy-start(f32[1024]{0:T(1024)} %param.30) | copy-start | bytes 12292
  77.6 126.1 %all-gather.9.cloned.1.call-start = ((), (), s32[]{:S(2)}) async-start(), calls=%async_computation.9 | async-start | bytes 2621440 | tf_op jit(solution)/shard_map/all_gather | solution.py:115
  78.1 163.9 %all-reduce.10.cloned.1.call-start = ((), (), s32[]{:S(2)}) async-start(), calls=%async_computation.10 | async-start | bytes 1048576 | tf_op jit(solution)/shard_map/psum | solution.py:177
  79.5 164.7 %copy-start.35 = (f32[256]{0:T(256)}, f32[256]{0:T(256)S(1)}, u32[]{:S(2)}) copy-start(f32[256]{0:T(256)S(1)} %compare_convert_fusion) | copy-start | bytes 3076
  111.7 132.5 %copy-start.29 = (f32[256]{0:T(256)}, f32[256]{0:T(256)S(1)}, u32[]{:S(2)}) copy-start(f32[256]{0:T(256)S(1)} %broadcast_multiply_fusion.4) | copy-start | bytes 3076
  112.0 132.3 %copy-start.34 = (f32[256]{0:T(256)}, f32[256]{0:T(256)S(1)}, u32[]{:S(2)}) copy-start(f32[256]{0:T(256)S(1)} %add_rsqrt_fusion) | copy-start | bytes 3076
  112.0 91.7 %copy-start.12 = (f32[1,256,1024]{2,1,0:T(8,128)S(1)}, f32[1,256,1024]{2,1,0:T(8,128)}, u32[]{:S(2)}) copy-start(f32[1,256,1024]{2,1,0:T(8,128)} %param.33) | copy-start | bytes 3145732
  209.7 68.0 %reduce-scatter.9.cloned.1.call-start = ((), (), s32[]{:S(2)}) async-start(), calls=%async_computation.12 | async-start | bytes 393216 | tf_op jit(solution)/shard_map/reduce_scatter | solution.py:236
  265.6 26.6 %reduce-scatter.7.cloned.1.call-start = ((), (), s32[]{:S(2)}) async-start(), calls=%async_computation.11 | async-start | bytes 393216 | tf_op jit(solution)/shard_map/reduce_scatter | solution.py:233
  269.9 47.1 %reduce-scatter.13.cloned.1.call-start = ((), (), s32[]{:S(2)}) async-start(), calls=%async_computation.14 | async-start | bytes 655360 | tf_op jit(solution)/shard_map/reduce_scatter | solution.py:289
  271.1 81.8 %reduce-scatter.11.cloned.1.call-start = ((), (), s32[]{:S(2)}) async-start(), calls=%async_computation.13 | async-start | bytes 1966080 | tf_op jit(solution)/shard_map/reduce_scatter | solution.py:286
  299.0 98.6 %reduce-scatter.15.cloned.1.call-start = ((), (), s32[]{:S(2)}) async-start(), calls=%async_computation.15 | async-start | bytes 2621440 | tf_op jit(solution)/shard_map/reduce_scatter | solution.py:292
  302.5 140.2 %reduce-scatter.17.cloned.1.call-start = ((), (), s32[]{:S(2)}) async-start(), calls=%async_computation.16 | async-start | bytes 2621440 | tf_op jit(solution)/shard_map/reduce_scatter | solution.py:295
  306.3 175.4 %all-reduce.12.cloned.1.call-start = ((), (), s32[]{:S(2)}) async-start(), calls=%async_computation.17 | async-start | bytes 2097152 | tf_op jit(solution)/shard_map/psum | solution.py:166
  311.4 132.8 %copy-start.18 = (bf16[256,256]{1,0:T(8,128)(2,1)S(1)}, bf16[256,256]{1,0:T(8,128)(2,1)}, u32[]{:S(2)}) copy-start(bf16[256,256]{1,0:T(8,128)(2,1)} %reduce-scatter.9.cloned.1.call-done) | copy-start | bytes 393220
  311.4 170.3 %copy-start.32 = (f32[256]{0:T(256)S(1)}, f32[256]{0:T(256)}, u32[]{:S(2)}) copy-start(f32[256]{0:T(256)} %copy-done.31) | copy-start | bytes 3076
  311.4 171.9 %copy-start.33 = (f32[1024]{0:T(1024)S(1)}, f32[1024]{0:T(1024)}, u32[]{:S(2)}) copy-start(f32[1024]{0:T(1024)} %get-tuple-element.424) | copy-start | bytes 12292
  311.4 225.7 %all-reduce.14.cloned.1.call-start = ((), (), s32[]{:S(2)}) async-start(), calls=%async_computation.18 | async-start | bytes 3145728 | tf_op jit(solution)/shard_map/psum | solution.py:300
  (37 other events, 350.2 us)
Sparse Core Ops, SparseCore 0:
  9.6 42.5 all-gather.4
  76.9 33.4 all-reduce.7
  112.0 45.7 all-gather.6
  159.2 44.4 all-gather.8
  209.8 32.2 all-reduce.9
  265.7 11.8 reduce-scatter.8
  280.4 11.7 reduce-scatter.6
  295.1 21.8 reduce-scatter.12
  319.3 33.5 reduce-scatter.10
  355.1 42.4 reduce-scatter.14
  399.9 42.8 reduce-scatter.16
  446.1 35.5 all-reduce.11
  484.2 52.9 all-reduce.13
where the time goes:
time: 552 us; the launch traced here: 551 us
  waiting for transfers between devices  374 us (68%)
  blocking collectives  72.5 us (13%)
  matrix products  36 us (7%)
  other arithmetic  30.6 us (6%)
  local copies, waits for them, and re-layouts  22.4 us (4%)
  between operations  14.4 us (3%)
    all_gather x1, waiting for transfers between devices, local(): lax.all_gather(up_weight, 'fsdp', axis=0, tiled=True)  45.8 us
    reduce_scatter x1, waiting for transfers between devices, local(): lax.psum_scatter(weight_terms[3].astype(jnp.bfloat16), 'fsdp', scatter_di...  45.2 us
    reduce_scatter x1, waiting for transfers between devices, local(): lax.psum_scatter(weight_terms[2].astype(jnp.bfloat16), 'fsdp', scatter_di...  44.6 us
    all_gather x1, waiting for transfers between devices, local(): lax.all_gather(down_weight, 'fsdp', axis=0, tiled=True)  42.6 us
    psum x1, blocking collectives, local(): lax.psum((small_terms[0], small_terms[1], small_terms[2], small_terms[3],...  38.9 us
    psum x1, waiting for transfers between devices, local(): lax.psum(mlp_part.astype(jnp.bfloat16), 'tensor').astype(jnp.float32)  37.4 us
    reduce_scatter x1, waiting for transfers between devices, local(): lax.psum_scatter(weight_terms[0].astype(jnp.bfloat16), 'fsdp', scatter_di...  36 us
    psum x1, waiting for transfers between devices, local(): lax.psum(jnp.dot(grad_u_b, up_full.T, preferred_element_type=jnp.float32)...  31.7 us
  transfers between devices with their start and end apart: 13, of which 13 were waited for; matrix products, arithmetic and copies ran while one was open for 7% of the time, Pallas kernels for 0%

commit v1 on v0

--- a/solution.py
+++ b/solution.py
@@ -174,9 +174,12 @@
     )
     grad_u_b = hidden_gradient.astype(jnp.bfloat16)
     up_weight_gradient = jnp.dot(norm2_b.T, grad_u_b, preferred_element_type=jnp.float32)
-    second_norm_gradient = lax.psum(
-        jnp.dot(grad_u_b, up_full.T, preferred_element_type=jnp.float32).astype(jnp.bfloat16),
-        "tensor",
+    second_norm_gradient = jnp.sum(
+        lax.all_gather(
+            jnp.dot(grad_u_b, up_full.T, preferred_element_type=jnp.float32).astype(jnp.bfloat16),
+            "tensor",
+        ),
+        axis=0,
     ).astype(jnp.float32)
     residual_gradient = result_gradient + layer_norm_backward(
         second_norm_gradient, second_normalized, second_inverse_deviation, middle_norm_gain

time: 552 us -> 541 us (0.980)
  waiting for transfers between devices: 374 us -> 362 us
    psum x1 -> x0, waiting for transfers between devices: 31.7 us -> none  [local(): lax.psum(jnp.dot(grad_u_b, up_full.T, preferred_element_type=jnp.float32)...]
    all_gather x0 -> x1, waiting for transfers between devices: none -> 20.8 us  [local(): lax.all_gather(jnp.dot(grad_u_b, up_full.T, preferred_element_type=jnp.fl...]
    reduce_scatter x1, waiting for transfers between devices: 5.53 us -> 12.9 us  [local(): lax.psum_scatter(weight_terms[1].astype(jnp.bfloat16), 'fsdp', scatter_di...]
    reduce_scatter x1, waiting for transfers between devices: 6.37 us -> 0.02 us  [local(): lax.psum_scatter(value_terms.astype(jnp.bfloat16), 'context', scatter_dim...]
  transfers between devices with their start and end apart: 13 -> 13, of which waited for: 13 -> 12; matrix products, arithmetic and copies ran while one was open for 7% -> 7% of each run, Pallas kernels for 0% -> 0%
where the time goes in v1:
time: 541 us; the launch traced here: 540 us
  waiting for transfers between devices  362 us (67%)
  blocking collectives  72.5 us (13%)
  matrix products  35.9 us (7%)
  other arithmetic  31.1 us (6%)
  local copies, waits for them, and re-layouts  23.2 us (4%)
  between operations  14.5 us (3%)
    all_gather x1, waiting for transfers between devices, local(): lax.all_gather(up_weight, 'fsdp', axis=0, tiled=True)  45.8 us
    reduce_scatter x1, waiting for transfers between devices, local(): lax.psum_scatter(weight_terms[3].astype(jnp.bfloat16), 'fsdp', scatter_di...  45 us
    reduce_scatter x1, waiting for transfers between devices, local(): lax.psum_scatter(weight_terms[2].astype(jnp.bfloat16), 'fsdp', scatter_di...  44.2 us
    all_gather x1, waiting for transfers between devices, local(): lax.all_gather(down_weight, 'fsdp', axis=0, tiled=True)  42.6 us
    psum x1, blocking collectives, local(): lax.psum((small_terms[0], small_terms[1], small_terms[2], small_terms[3],...  38.9 us
    psum x1, waiting for transfers between devices, local(): lax.psum(mlp_part.astype(jnp.bfloat16), 'tensor').astype(jnp.float32)  37.1 us
    reduce_scatter x1, waiting for transfers between devices, local(): lax.psum_scatter(weight_terms[0].astype(jnp.bfloat16), 'fsdp', scatter_di...  37 us
    psum x1, waiting for transfers between devices, local(): lax.psum(attn_part.astype(jnp.bfloat16), 'tensor').astype(jnp.float32)  30.9 us
  transfers between devices with their start and end apart: 13, of which 12 were waited for; matrix products, arithmetic and copies ran while one was open for 7% of the time, Pallas kernels for 0%

profile of v1, /device:TPU:0, one launch (start us, length us, event | category | flops | bytes accessed | tf_op | source)
XLA Modules:
  0.0 540.0 jit_solution(86515955152762801)
XLA Ops:
  10.6 22.1 %all_gather.29 = bf16[1024,256]{1,0:T(8,128)(2,1)S(1)} all-gather(bf16[256,256]{1,0:T(8,128)(2,1)S(1)} %copy-done.23), channel_id=1, replica_groups=mesh['fsdp'=4,'context'=2,'tensor'=4] {'fsdp'}, dimensions={0}, use_global_device_ids=true | all-gather | bytes 655360 | tf_op jit(solution)/shard_map/all_gather | solution.py:113
  32.6 19.6 %all-gather.7.cloned.1.call-done = bf16[1024,3,256]{2,0,1:T(8,128)(2,1)} async-done(((bf16[256,3,256]{2,0,1:T(8,128)(2,1)}), bf16[1024,3,256]{2,0,1:T(8,128)(2,1)}) %all-gather.7.cloned.1.call-update) | async-done | bytes 1572880 | tf_op jit(solution)/shard_map/all_gather | solution.py:112
  57.1 6.0 %all_gather.28 = bf16[512,256]{0,1:T(8,128)(2,1)S(1)} all-gather(bf16[256,256]{0,1:T(8,128)(2,1)S(1)} %fusion.75), channel_id=1, replica_groups=mesh['fsdp'=4,'context'=2,'tensor'=4] {'context'}, dimensions={0}, use_global_device_ids=true | all-gather | bytes 393216 | tf_op jit(solution)/shard_map/all_gather | solution.py:141
  63.2 5.6 %all-gather = bf16[512,1,256]{0,2,1:T(8,128)(2,1)S(1)} all-gather(bf16[256,1,256]{0,2,1:T(8,128)(2,1)S(1)} %slice.31), channel_id=2, replica_groups=mesh['fsdp'=4,'context'=2,'tensor'=4] {'context'}, dimensions={0}, use_global_device_ids=true | all-gather | bytes 393216 | tf_op jit(solution)/shard_map/all_gather | solution.py:140
  69.0 5.9 %while.34 = (s32[]{:T(128)}, f32[256,4]{0,1:T(4,128)S(1)}, f32[256,4]{0,1:T(4,128)S(1)}, f32[256,4,64]{0,2,1:T(8,128)S(1)}, s32[2]{0:T(128)S(1)}, /*index=5*/s32...) while((s32[]{:T(128)}, f32[256,4]{0,1:T(4,128)S(1)}, ...), condition=%wide.region_7.8_spmd.clone, body=%wide.region_3.7_spmd.clone.sunk | while | flops 69678592 | bytes 4134565 | solution.py:80
  79.4 30.9 %all-reduce.7.cloned.1.call-done = bf16[256,1024]{1,0:T(8,128)(2,1)} async-done(((bf16[256,1024]{1,0:T(8,128)(2,1)}), bf16[256,1024]{1,0:T(8,128)(2,1)}) %all-reduce.7.cloned.1.call-update) | async-done | bytes 524304 | tf_op jit(solution)/shard_map/psum | solution.py:154
  111.9 45.8 %all-gather.9.cloned.1.call-done = bf16[1024,1024]{1,0:T(8,128)(2,1)} async-done(((bf16[256,1024]{1,0:T(8,128)(2,1)}), bf16[1024,1024]{1,0:T(8,128)(2,1)}) %all-gather.9.cloned.1.call-update) | async-done | bytes 2097168 | tf_op jit(solution)/shard_map/all_gather | solution.py:114
  157.7 3.3 convolution_add_fusion
  161.0 42.6 %all-gather.11.cloned.1.call-done = bf16[1024,1024]{1,0:T(8,128)(2,1)} async-done(((bf16[256,1024]{1,0:T(8,128)(2,1)}), bf16[1024,1024]{1,0:T(8,128)(2,1)}) %all-gather.11.cloned.1.call-update) | async-done | bytes 2097168 | tf_op jit(solution)/shard_map/all_gather | solution.py:115
  203.6 3.6 fusion.92
  210.2 20.8 %all-gather.13.cloned.1.call-done = bf16[1024,1024]{1,0:T(8,128)(2,1)} async-done(((bf16[256,1024]{1,0:T(8,128)(2,1)}), bf16[1024,1024]{1,0:T(8,128)(2,1)}) %all-gather.13.cloned.1.call-update) | async-done | bytes 2097168 | tf_op jit(solution)/shard_map/all_gather | solution.py:178
  237.0 14.0 %while.35 = (s32[]{:T(128)}, f32[256,4,64]{0,2,1:T(8,128)}, bf16[2,256,4,64]{1,3,2,0:T(8,128)(2,1)}, bf16[2,256,4,64]{1,3,2,0:T(8,128)(2,1)}, bf16[2,256,4,64]{1...) while((s32[]{:T(128)}, f32[256,4,64]{0,2,1:T(8,128)}, ...), condition=%wide.region_18.19_spmd.clone, body=%wide.region_16.18_spmd.clone.sunk | while | flops 169878016 | bytes 12989295 | solution.py:228
  260.8 3.2 convolution_convert_fusion.1
  264.3 3.7 convolution_convert_fusion
  269.1 12.6 %reduce-scatter.7.cloned.1.call-done = bf16[256,256]{1,0:T(8,128)(2,1)} async-done(((bf16[512,256]{1,0:T(8,128)(2,1)}), bf16[256,256]{1,0:T(8,128)(2,1)}) %reduce-scatter.7.cloned.1.call-update) | async-done | bytes 131088 | tf_op jit(solution)/shard_map/reduce_scatter | solution.py:236
  285.4 3.0 convolution_convert_fusion.2
  288.5 3.6 convolution_convert_fusion.6
  293.5 12.9 %reduce-scatter.13.cloned.1.call-done = bf16[256,256]{1,0:T(8,128)(2,1)} async-done(((bf16[1024,256]{1,0:T(8,128)(2,1)}), bf16[256,256]{1,0:T(8,128)(2,1)}) %reduce-scatter.13.cloned.1.call-update) | async-done | bytes 131088 | tf_op jit(solution)/shard_map/reduce_scatter | solution.py:292
  306.4 44.2 %reduce-scatter.15.cloned.1.call-done = bf16[256,1024]{1,0:T(8,128)(2,1)} async-done(((bf16[1024,1024]{1,0:T(8,128)(2,1)}), bf16[256,1024]{1,0:T(8,128)(2,1)}) %reduce-scatter.15.cloned.1.call-update) | async-done | bytes 524304 | tf_op jit(solution)/shard_map/reduce_scatter | solution.py:295
  350.6 45.0 %reduce-scatter.17.cloned.1.call-done = bf16[256,1024]{1,0:T(8,128)(2,1)} async-done(((bf16[1024,1024]{1,0:T(8,128)(2,1)}), bf16[256,1024]{1,0:T(8,128)(2,1)}) %reduce-scatter.17.cloned.1.call-update) | async-done | bytes 524304 | tf_op jit(solution)/shard_map/reduce_scatter | solution.py:298
  395.6 37.0 %reduce-scatter.11.cloned.1.call-done = bf16[256,3,256]{2,0,1:T(8,128)(2,1)} async-done(((bf16[1024,3,256]{2,0,1:T(8,128)(2,1)}), bf16[256,3,256]{2,0,1:T(8,128)(2,1)}) %reduce-scatter.11.cloned.1.call-update) | async-done | bytes 393232 | tf_op jit(solution)/shard_map/reduce_scatter | solution.py:289
  434.1 37.1 %all-reduce.9.cloned.1.call-done = (bf16[256,1024]{1,0:T(8,128)(2,1)}, bf16[256,1024]{1,0:T(8,128)(2,1)}) async-done(((bf16[256,1024]{1,0:T(8,128)(2,1)}, bf16[256,1024]{1,0:T(8,128)(2,1)}), (bf16[256,1024]{1,0:T(8,128)(2,1)}, bf16[256,1024]{1,0:T(8,128)(2,1)})) %all-reduce.9.cloned.1.call-update) | async-done | bytes 1048592 | tf_op jit(solution)/shard_map/psum | solution.py:166
  472.8 38.9 %all-reduce = (f32[1024]{0:T(1024)}, f32[1024]{0:T(1024)}, f32[2,256]{1,0:T(2,128)}, f32[1024]{0:T(1024)}, f32[1024]{0:T(1024)}, /*index=5*/f32[1024]{0:T(1024)}, f32[1024]{0:T(1024)}, f32[1024]{0:T(1024)}) all-reduce(f32[1024]{0:T(1024)S(1)} %get-tuple-element.426, ...), channel_id=1, replica_groups=mesh['fsdp'=4,'context'=2,'tensor'=4] {'fsdp','context'}, use_global_device_ids=true, to_apply=%region_25.26 | all-reduce | flops 7680 | bytes 61440 | tf_op jit(solution)/shard_map/psum | solution.py:269
  515.3 11.4 %all-reduce.11.cloned.1.call-done = (bf16[256,3,256]{2,0,1:T(8,128)(2,1)}, bf16[256,256]{1,0:T(8,128)(2,1)}, bf16[256,1024]{1,0:T(8,128)(2,1)}, bf16[256,1024]{1,0:T(8,128)(2,1)}) async-done(((bf16[256,3,256]{2,0,1:T(8,128)(2,1)}, bf16[256,256]{1,0:T(8,128)(2,1)}, bf16[256,1024]{1,0:T(8,128)(2,1)}, bf16[256,1024]{1,0:T(8,128)(2,1)}), (bf16[256,3,256]{2,0,1:T(8,128)(2,1)}, bf16[256,256]{1,0:T(8,128)(2,1)}, ...) | async-done | bytes 1572880 | tf_op jit(solution)/shard_map/psum | solution.py:303
  (233 shorter events, 72.5 us)
Async XLA Ops:
  7.2 45.0 %all-gather.7.cloned.1.call-start = ((), (), s32[]{:S(2)}) async-start(), calls=%async_computation.6 | async-start | bytes 1966080 | tf_op jit(solution)/shard_map/all_gather | solution.py:112
  7.9 102.3 %all-reduce.7.cloned.1.call-start = ((), (), s32[]{:S(2)}) async-start(), calls=%async_computation.7 | async-start | bytes 1048576 | tf_op jit(solution)/shard_map/psum | solution.py:154
  10.3 44.5 %copy-start.29 = (f32[256]{0:T(256)}, f32[256]{0:T(256)S(1)}, u32[]{:S(2)}) copy-start(f32[256]{0:T(256)S(1)} %broadcast_multiply_fusion.5) | copy-start | bytes 3076
  10.5 44.2 %copy-start.26 = (f32[1024]{0:T(1024)S(1)}, f32[1024]{0:T(1024)}, u32[]{:S(2)}) copy-start(f32[1024]{0:T(1024)} %param.21) | copy-start | bytes 12292
  76.7 81.0 %all-gather.9.cloned.1.call-start = ((), (), s32[]{:S(2)}) async-start(), calls=%async_computation.8 | async-start | bytes 2621440 | tf_op jit(solution)/shard_map/all_gather | solution.py:114
  77.4 80.2 %copy-start.27 = (f32[1024]{0:T(1024)S(1)}, f32[1024]{0:T(1024)}, u32[]{:S(2)}) copy-start(f32[1024]{0:T(1024)} %param.27) | copy-start | bytes 12292
  77.4 80.2 %copy-start.41 = (f32[1024]{0:T(1024)S(1)}, f32[1024]{0:T(1024)}, u32[]{:S(2)}) copy-start(f32[1024]{0:T(1024)} %param.28) | copy-start | bytes 12292
  77.4 80.2 %copy-start.46 = (f32[1024]{0:T(1024)S(1)}, f32[1024]{0:T(1024)}, u32[]{:S(2)}) copy-start(f32[1024]{0:T(1024)} %param.30) | copy-start | bytes 12292
  77.5 126.1 %all-gather.11.cloned.1.call-start = ((), (), s32[]{:S(2)}) async-start(), calls=%async_computation.9 | async-start | bytes 2621440 | tf_op jit(solution)/shard_map/all_gather | solution.py:115
  78.0 153.0 %all-gather.13.cloned.1.call-start = ((), (), s32[]{:S(2)}) async-start(), calls=%async_computation.16 | async-start | bytes 2621440 | tf_op jit(solution)/shard_map/all_gather | solution.py:178
  79.4 154.8 %copy-start.38 = (f32[256]{0:T(256)}, f32[256]{0:T(256)S(1)}, u32[]{:S(2)}) copy-start(f32[256]{0:T(256)S(1)} %compare_convert_fusion) | copy-start | bytes 3076
  111.6 122.6 %copy-start.31 = (f32[256]{0:T(256)}, f32[256]{0:T(256)S(1)}, u32[]{:S(2)}) copy-start(f32[256]{0:T(256)S(1)} %broadcast_multiply_fusion.4) | copy-start | bytes 3076
  111.8 122.4 %copy-start.36 = (f32[256]{0:T(256)}, f32[256]{0:T(256)S(1)}, u32[]{:S(2)}) copy-start(f32[256]{0:T(256)S(1)} %add_rsqrt_fusion) | copy-start | bytes 3076
  111.8 91.7 %copy-start.13 = (f32[1,256,1024]{2,1,0:T(8,128)S(1)}, f32[1,256,1024]{2,1,0:T(8,128)}, u32[]{:S(2)}) copy-start(f32[1,256,1024]{2,1,0:T(8,128)} %param.33) | copy-start | bytes 3145732
  209.5 59.5 %reduce-scatter.9.cloned.1.call-start = ((), (), s32[]{:S(2)}) async-start(), calls=%async_computation.11 | async-start | bytes 393216 | tf_op jit(solution)/shard_map/reduce_scatter | solution.py:239
  255.2 26.5 %reduce-scatter.7.cloned.1.call-start = ((), (), s32[]{:S(2)}) async-start(), calls=%async_computation.10 | async-start | bytes 393216 | tf_op jit(solution)/shard_map/reduce_scatter | solution.py:236
  259.5 47.0 %reduce-scatter.13.cloned.1.call-start = ((), (), s32[]{:S(2)}) async-start(), calls=%async_computation.13 | async-start | bytes 655360 | tf_op jit(solution)/shard_map/reduce_scatter | solution.py:292
  260.7 89.9 %reduce-scatter.15.cloned.1.call-start = ((), (), s32[]{:S(2)}) async-start(), calls=%async_computation.14 | async-start | bytes 2621440 | tf_op jit(solution)/shard_map/reduce_scatter | solution.py:295
  264.0 131.6 %reduce-scatter.17.cloned.1.call-start = ((), (), s32[]{:S(2)}) async-start(), calls=%async_computation.15 | async-start | bytes 2621440 | tf_op jit(solution)/shard_map/reduce_scatter | solution.py:298
  268.0 164.5 %reduce-scatter.11.cloned.1.call-start = ((), (), s32[]{:S(2)}) async-start(), calls=%async_computation.12 | async-start | bytes 1966080 | tf_op jit(solution)/shard_map/reduce_scatter | solution.py:289
  288.4 182.8 %all-reduce.9.cloned.1.call-start = ((), (), s32[]{:S(2)}) async-start(), calls=%async_computation.17 | async-start | bytes 2097152 | tf_op jit(solution)/shard_map/psum | solution.py:166
  293.5 140.6 %copy-start.20 = (bf16[256,256]{1,0:T(8,128)(2,1)S(1)}, bf16[256,256]{1,0:T(8,128)(2,1)}, u32[]{:S(2)}) copy-start(bf16[256,256]{1,0:T(8,128)(2,1)} %reduce-scatter.9.cloned.1.call-done) | copy-start | bytes 393220
  293.5 179.3 %copy-start.35 = (f32[1024]{0:T(1024)S(1)}, f32[1024]{0:T(1024)}, u32[]{:S(2)}) copy-start(f32[1024]{0:T(1024)} %get-tuple-element.424) | copy-start | bytes 12292
  293.5 233.2 %all-reduce.11.cloned.1.call-start = ((), (), s32[]{:S(2)}) async-start(), calls=%async_computation.18 | async-start | bytes 3145728 | tf_op jit(solution)/shard_map/psum | solution.py:303
  (43 other events, 347.9 us)
Sparse Core Ops, SparseCore 0:
  9.6 42.5 all-gather.6
  76.8 33.4 all-reduce.6
  111.8 45.7 all-gather.8
  159.1 44.4 all-gather.10
  209.7 21.3 all-gather.12
  255.3 11.7 reduce-scatter.8
  269.9 11.7 reduce-scatter.6
  284.5 21.8 reduce-scatter.12
  308.7 41.8 reduce-scatter.14
  352.8 42.8 reduce-scatter.16
  397.9 34.6 reduce-scatter.10
  436.0 35.1 all-reduce.8
  473.7 52.9 all-reduce.10
